TPU v7x, 256 devices: a whole 4x4x8 slice. The times are simulated.
256 devices in a mesh: stream: 2 (over z_hi), dp: 16 (over x, y), tensor: 8 (over z_lo, core).
Axes of the slice: x: 4, y: 4, z: 8 (z_hi: 2, z_lo: 4; z = z_hi * 4 + z_lo), core: 2. Of those that a mesh axis runs over, the one named last changes fastest.
Arguments:
- hidden: bfloat16 [2, 256, 8192], P('stream', 'tensor', 'dp'), may hold values from -3 to 3
- cached_rotated_keys: bfloat16 [2, 256, 8, 256, 128], P('stream', 'dp', 'tensor'), may hold values from -6 to 6
- cached_values: bfloat16 [2, 256, 8, 256, 128], P('stream', 'dp', 'tensor'), may hold values from -18 to 18
- cache_lengths: int32 [2, 256], P('stream', 'dp'), may hold values from 1 to 256, as said below
- recent_ids: int32 [256, 128], replicated, may hold values from 0 to 65535
- guidance: float32 [256], replicated, may hold values from 1 to 3
- w_query: bfloat16 [8192, 8192], P('dp', 'tensor'), may hold values from -0.0625 to 0.0625
- key_value_weight: bfloat16 [8192, 2, 1024], P('dp', None, 'tensor'), may hold values from -0.0625 to 0.0625
- w_output: bfloat16 [8192, 8192], P('tensor', 'dp'), may hold values from -0.0625 to 0.0625
- norm_gain: bfloat16 [8192], P('dp'), may hold values from 0.5 to 1.5
- w_head: bfloat16 [8192, 65536], P(None, ('dp', 'tensor')), may hold values from -0.16503906 to 0.16503906
Outputs:
- guided_logprobs: float32 [256, 65536], P('stream', ('dp', 'tensor'))
Inputs may be any that keep to these rules, and one draw needn't show every extreme that they name: `cache_lengths`: every prompt has 1 to 256 filled slots in each stream; some prompt has all 256; lengths differ widely from one group of 16 prompts to the next.
All inputs are finite; a program needn't handle non-finite values.
Results may differ from a plain program's by a relative error of at most 0.0025.
Values may be sent and summed in bfloat16 or wider, within the bound.
A program may use at most 64 MiB of HBM per device.

v0:
```python
import jax
import jax.numpy as jnp
from jax import lax
from jax.sharding import PartitionSpec as P

MODEL_WIDTH = 8192
HEAD_SIZE = 128
rope_theta = 500000.0
penalty_step = 1.5
norm_eps = 1e-05


def partner_2(value, axis, distance):
    mask = 2**distance
    pairs = [(source, source ^ mask) for source in range(lax.axis_size(axis))]
    return lax.ppermute(value, axis, pairs)


def rotate(values, positions):
    halfway = values.shape[-1] // 2
    frequency = rope_theta ** (-(jnp.arange(halfway, dtype=jnp.float32) * 2.0 / values.shape[-1]))
    angles = positions.astype(jnp.float32)[:, None, None] * frequency
    cosine_term = jnp.cos(angles)
    sine_term = jnp.sin(angles)
    first_half = values[..., :halfway]
    second_half = values[..., halfway:]
    return jnp.concatenate(
        [
            first_half * cosine_term - second_half * sine_term,
            second_half * cosine_term + first_half * sine_term,
        ],
        axis=-1,
    )


def repeat_counts(recent_ids, first_column, width):
    columns = first_column + jnp.arange(width, dtype=jnp.int32)
    return jnp.sum((recent_ids[:, :, None] == columns[None, None, :]).astype(jnp.float32), 1)


def body(
    hidden,
    cached_rotated_keys,
    cached_values,
    cache_lengths,
    recent_ids,
    guidance,
    w_query,
    key_value_weight,
    w_output,
    norm_gain,
    w_head,
):
    local_width = hidden.shape[2]
    query_cols = w_query.shape[1]
    kv_cols = key_value_weight.shape[2]
    local_prompts = cache_lengths.shape[1]
    lengths = cache_lengths[0]
    vocab_local = w_head.shape[1]
    all_rows = lax.all_gather(hidden[0], "tensor", axis=0, tiled=True)
    kv_flat = key_value_weight.reshape(local_width, 2 * kv_cols)
    projected = lax.psum_scatter(
        jnp.concatenate(
            [
                jnp.dot(all_rows, w_query, preferred_element_type=jnp.float32),
                jnp.dot(all_rows, kv_flat, preferred_element_type=jnp.float32),
            ],
            axis=1,
        ),
        "dp",
        scatter_dimension=0,
        tiled=True,
    )
    query_heads = query_cols // HEAD_SIZE
    kv_heads = kv_cols // HEAD_SIZE
    rotated_query = rotate(
        projected[:, :query_cols].reshape(local_prompts, query_heads, HEAD_SIZE), lengths
    ).astype(jnp.bfloat16)
    key_value_rows = projected[:, query_cols:].reshape(local_prompts, 2, kv_heads, HEAD_SIZE)
    fresh_key = rotate(key_value_rows[:, 0], lengths).astype(jnp.bfloat16)
    value_new = key_value_rows[:, 1].astype(jnp.bfloat16)
    grouped_queries = rotated_query.reshape(
        local_prompts, kv_heads, query_heads // kv_heads, HEAD_SIZE
    )
    attention_scale = HEAD_SIZE ** (-0.5)
    key_block = cached_rotated_keys[0]
    value_block = cached_values[0]
    scores = (
        jnp.einsum(
            "pkgd,pksd->pkgs", grouped_queries, key_block, preferred_element_type=jnp.float32
        )
        * attention_scale
    )
    self_score = (
        jnp.einsum("pkgd,pkd->pkg", grouped_queries, fresh_key, preferred_element_type=jnp.float32)
        * attention_scale
    )
    valid = jnp.arange(key_block.shape[2], dtype=jnp.int32)[None, :] < lengths[:, None]
    exps = jnp.where(valid[:, None, None, :], jnp.exp(scores), 0.0)
    own_exp = jnp.exp(self_score)
    denominator = jnp.sum(exps, -1) + own_exp
    weights = (exps / denominator[..., None]).astype(jnp.bfloat16)
    own_weight = (own_exp / denominator).astype(jnp.bfloat16)
    attended = jnp.einsum(
        "pkgs,pksd->pkgd", weights, value_block, preferred_element_type=jnp.float32
    )
    attended = (
        attended
        + own_weight.astype(jnp.float32)[..., None] * value_new.astype(jnp.float32)[:, :, None, :]
    )
    attended = attended.reshape(local_prompts, query_cols).astype(jnp.bfloat16)
    partial_out = jnp.dot(
        lax.all_gather(attended, "dp", axis=0, tiled=True),
        w_output,
        preferred_element_type=jnp.float32,
    )
    output_sum = lax.psum_scatter(partial_out, "tensor", scatter_dimension=0, tiled=True)
    residual = (hidden[0].astype(jnp.float32) + output_sum).astype(jnp.bfloat16)
    widened = residual.astype(jnp.float32)
    squares = lax.psum(jnp.sum(widened * widened, 1), "dp")
    inverse = lax.rsqrt(squares / MODEL_WIDTH + norm_eps)
    normed = (widened * inverse[:, None] * norm_gain.astype(jnp.float32)).astype(jnp.bfloat16)
    normed_all = lax.all_gather(normed, "tensor", axis=0, tiled=True)
    logits = jnp.dot(
        lax.all_gather(normed_all, "dp", axis=1, tiled=True),
        w_head,
        preferred_element_type=jnp.float32,
    )
    stream_side = lax.axis_index("stream")
    half_rows = logits.shape[0] // 2
    mine_start = stream_side * half_rows
    other_start = (1 - stream_side) * half_rows
    column_base = lax.axis_index(("dp", "tensor")) * vocab_local
    mine = lax.dynamic_slice_in_dim(logits, mine_start, half_rows, 0)
    sending = lax.dynamic_slice_in_dim(logits, other_start, half_rows, 0)
    partner = partner_2(sending, "stream", 0)
    conditional = jnp.where(stream_side == 0, mine, partner)
    unconditional = jnp.where(stream_side == 0, partner, mine)
    guide = lax.dynamic_slice_in_dim(guidance, mine_start, half_rows, 0)[:, None]
    recent_mine = lax.dynamic_slice_in_dim(recent_ids, mine_start, half_rows, 0)
    guided = unconditional + guide * (conditional - unconditional)
    guided = guided - penalty_step * repeat_counts(recent_mine, column_base, vocab_local)
    totals = lax.psum(jnp.sum(jnp.exp(guided), 1), ("dp", "tensor"))
    return guided - jnp.log(totals)[:, None]


def solution(mesh):
    return jax.shard_map(
        body,
        mesh=mesh,
        in_specs=(
            P("stream", "tensor", "dp"),
            P("stream", "dp", "tensor", None, None),
            P("stream", "dp", "tensor", None, None),
            P("stream", "dp"),
            P(),
            P(),
            P("dp", "tensor"),
            P("dp", None, "tensor"),
            P("tensor", "dp"),
            P("dp"),
            P(None, ("dp", "tensor")),
        ),
        out_specs=P("stream", ("dp", "tensor")),
        check_vma=False,
    )
```

profile of v0, /device:TPU:128, one launch (start us, length us, event | category | flops | bytes accessed | tf_op | source)
XLA Modules:
  0.0 647.4 jit_solution(1154850240006349418)
XLA Ops:
  6.6 14.5 %all-gather = bf16[1,256,512]{2,1,0:T(8,128)(2,1)S(1)} all-gather(bf16[1,32,512]{2,1,0:T(8,128)(2,1)} %param.11), channel_id=2, replica_groups=mesh['stream'=2,'dp'=16,'tensor'=8] {'tensor'}, dimensions={1}, use_global_device_ids=true | all-gather | bytes 294912 | tf_op jit(solution)/shard_map/all_gather | solution.py:60
  21.1 0.5 fusion.9
  21.6 1.2 fusion.5
  22.8 1.2 pad_maximum_fusion
  24.1 0.7 bitcast_convert_fusion
  24.7 0.7 iota_compare_fusion
  25.6 79.2 %reduce-scatter.3.cloned.1.call-done = f32[16,1280]{1,0:T(8,128)} async-done(((f32[256,1280]{1,0:T(8,128)}), f32[16,1280]{1,0:T(8,128)}) %reduce-scatter.3.cloned.1.call-update) | async-done | bytes 81936 | tf_op jit(solution)/shard_map/reduce_scatter | solution.py:62
  104.8 0.7 slice.36
  105.7 0.8 slice_bitcast_fusion
  106.9 1.7 fusion.33
  108.7 0.3 fusion.2
  109.0 23.3 %all_gather.13 = bf16[256,1024]{1,0:T(8,128)(2,1)S(1)} all-gather(bf16[16,1024]{1,0:T(8,128)(2,1)S(1)} %bitcast.51), channel_id=1, replica_groups=mesh['stream'=2,'dp'=16,'tensor'=8] {'dp'}, dimensions={0}, use_global_device_ids=true | all-gather | bytes 557056 | tf_op jit(solution)/shard_map/all_gather | solution.py:113
  132.3 1.2 fusion.34
  133.6 32.9 %reduce-scatter.5.cloned.1.call-done = f32[32,512]{1,0:T(8,128)} async-done(((f32[256,512]{1,0:T(8,128)}), f32[32,512]{1,0:T(8,128)}) %reduce-scatter.5.cloned.1.call-update) | async-done | bytes 65552 | tf_op jit(solution)/shard_map/reduce_scatter | solution.py:117
  166.5 1.0 fusion.11
  167.5 40.3 %psum.14 = f32[32]{0:T(128)S(1)} all-reduce(f32[32]{0:T(128)S(1)} %fusion.11), channel_id=1, replica_groups=mesh['stream'=2,'dp'=16,'tensor'=8] {'dp'}, use_global_device_ids=true, to_apply=%region_4.5 | all-reduce | flops 32 | bytes 256 | tf_op jit(solution)/shard_map/psum | solution.py:120
  207.8 0.9 fusion.13
  208.7 15.3 %all_gather.14 = bf16[256,512]{1,0:T(8,128)(2,1)} all-gather(bf16[32,512]{1,0:T(8,128)(2,1)S(1)} %fusion.13), channel_id=1, replica_groups=mesh['stream'=2,'dp'=16,'tensor'=8] {'tensor'}, dimensions={0}, use_global_device_ids=true | all-gather | bytes 294912 | tf_op jit(solution)/shard_map/all_gather | solution.py:123
  224.2 58.3 %all-gather.3.cloned.1.call-done = bf16[256,8192]{1,0:T(8,128)(2,1)} async-done(((bf16[256,512]{1,0:T(8,128)(2,1)}), bf16[256,8192]{1,0:T(8,128)(2,1)}) %all-gather.3.cloned.1.call-update) | async-done | bytes 4194320 | tf_op jit(solution)/shard_map/all_gather | solution.py:125
  282.5 7.0 %fusion.35 = f32[256,512]{1,0:T(8,128)S(1)} fusion(bf16[256,8192]{1,0:T(8,128)(2,1)} %all-gather.3.cloned.1.call-done, bf16[8192,512]{1,0:T(8,128)(2,1)} %param.21), kind=kOutput, calls=%fused_computation.66 | convolution fusion | flops 2147483648 | bytes 13107200 | tf_op jit(solution)/shard_map/dot_general | solution.py:124
  289.8 4.7 convert_reduce_fusion
  294.4 11.4 %collective-permute-done = f32[128,512]{1,0:T(8,128)S(1)} collective-permute-done((f32[128,512]{1,0:T(8,128)S(1)}, f32[128,512]{1,0:T(8,128)S(1)}, u32[]{:S(2)}, u32[]{:S(2)}) %collective-permute-start) | collective-permute-done | bytes 262176 | tf_op jit(solution)/shard_map/ppermute | solution.py:16
  306.0 334.1 %psum.15 = f32[128]{0:T(128)S(1)} all-reduce(f32[128]{0:T(128)S(1)} %get-tuple-element.5), channel_id=1, replica_groups=mesh['stream'=2,'dp'=16,'tensor'=8] {'dp','tensor'}, use_global_device_ids=true, to_apply=%region_7.8 | all-reduce | flops 128 | bytes 1024 | tf_op jit(solution)/shard_map/psum | solution.py:143
  640.1 0.8 broadcast_subtract_fusion
  (41 shorter events, 1.5 us)
Async XLA Ops:
  6.5 14.6 %copy-start = (bf16[512,1024]{1,0:T(8,128)(2,1)S(1)}, bf16[512,1024]{1,0:T(8,128)(2,1)}, u32[]{:S(2)}) copy-start(bf16[512,1024]{1,0:T(8,128)(2,1)} %param.17) | copy-start | bytes 3145732
  6.5 160.0 %copy-start.3 = (bf16[1,32,512]{2,1,0:T(8,128)(2,1)S(1)}, bf16[1,32,512]{2,1,0:T(8,128)(2,1)}, u32[]{:S(2)}) copy-start(bf16[1,32,512]{2,1,0:T(8,128)(2,1)} %param.11) | copy-start | bytes 98308
  6.5 102.2 %copy-start.1 = (bf16[1,16,1,256,128]{4,3,2,1,0:T(8,128)(2,1)S(1)}, bf16[1,16,1,256,128]{4,3,2,1,0:T(8,128)(2,1)}, u32[]{:S(2)}) copy-start(bf16[1,16,1,256,128]{4,3,2,1,0:T(8,128)(2,1)} %param.13) | copy-start | bytes 3145732
  6.5 125.8 %copy-start.2 = (bf16[1024,512]{1,0:T(8,128)(2,1)S(1)}, bf16[1024,512]{1,0:T(8,128)(2,1)}, u32[]{:S(2)}) copy-start(bf16[1024,512]{1,0:T(8,128)(2,1)} %param.19) | copy-start | bytes 3145732
  6.5 127.1 %copy-start.5 = (bf16[512]{0:T(512)(128)(2,1)S(1)}, bf16[512]{0:T(512)(128)(2,1)}, u32[]{:S(2)}) copy-start(bf16[512]{0:T(512)(128)(2,1)} %param.20) | copy-start | bytes 3076
  6.5 217.5 %copy-start.6 = (f32[256]{0:T(256)S(1)}, f32[256]{0:T(256)}, u32[]{:S(2)}) copy-start(f32[256]{0:T(256)} %param.16) | copy-start | bytes 3076
  6.6 217.6 %copy-start.4 = (s32[256,128]{1,0:T(8,128)S(1)}, s32[256,128]{1,0:T(8,128)}, u32[]{:S(2)}) copy-start(s32[256,128]{1,0:T(8,128)} %param.15) | copy-start | bytes 393220
  6.6 98.2 %reduce-scatter.3.cloned.1.call-start = ((), (), s32[]{:S(2)}) async-start(), calls=%async_computation.2 | async-start | bytes 1392640 | tf_op jit(solution)/shard_map/reduce_scatter | solution.py:62
  24.0 142.5 %reduce-scatter.5.cloned.1.call-start = ((), (), s32[]{:S(2)}) async-start(), calls=%async_computation.3 | async-start | bytes 589824 | tf_op jit(solution)/shard_map/reduce_scatter | solution.py:117
  133.6 148.9 %all-gather.3.cloned.1.call-start = ((), (), s32[]{:S(2)}) async-start(), calls=%async_computation.4 | async-start | bytes 4456448 | tf_op jit(solution)/shard_map/all_gather | solution.py:125
  289.5 16.3 %collective-permute-start = (f32[128,512]{1,0:T(8,128)S(1)}, f32[128,512]{1,0:T(8,128)S(1)}, u32[]{:S(2)}, u32[]{:S(2)}) collective-permute-start(f32[128,512]{1,0:T(8,128)S(1)} %constant_dynamic-slice_fusion.1), channel_id=1, source_target_pairs={{0,128},{128,0},{1,129},{129,1},{2,130},{130,2},{3,131},{131,3},{4... | collective-permute-start | bytes 786440 | tf_op jit(solution)/shard_map/ppermute | solution.py:16
Sparse Core Ops, SparseCore 0:
  24.1 80.6 reduce-scatter.2
  133.7 32.7 reduce-scatter.4
  224.2 58.2 all-gather.2
where the time goes:
time: 648 us; the launch traced here: 647 us
  blocking collectives  427 us (66%)
  waiting for transfers between devices  182 us (28%)
  between operations  13.3 us (2%)
  matrix products  12.1 us (2%)
  other arithmetic  10.5 us (2%)
    psum x1, blocking collectives, body(): totals = lax.psum(jnp.sum(jnp.exp(guided), 1), ('dp', 'tensor'))  334 us
    reduce_scatter x1, waiting for transfers between devices, body(): lax.psum_scatter(jnp.concatenate([jnp.dot(all_rows, w_query, preferred_el...  79.2 us
    all_gather x1, waiting for transfers between devices, body(): lax.all_gather(normed_all, 'dp', axis=1, tiled=True)  58.3 us
    psum x1, blocking collectives, body(): squares = lax.psum(jnp.sum(widened * widened, 1), 'dp')  40.3 us
    reduce_scatter x1, waiting for transfers between devices, body(): lax.psum_scatter(partial_out, 'tensor', scatter_dimension=0, tiled=True)  32.9 us
    all_gather x1, blocking collectives, body(): lax.all_gather(attended, 'dp', axis=0, tiled=True)  23.3 us
    all_gather x1, blocking collectives, body(): normed_all = lax.all_gather(normed, 'tensor', axis=0, tiled=True)  15.3 us
    all_gather x1, blocking collectives, body(): all_rows = lax.all_gather(hidden[0], 'tensor', axis=0, tiled=True)  14.5 us
  transfers between devices with their start and end apart: 4, of which 4 were waited for; matrix products, arithmetic and copies ran while one was open for 1% of the time, Pallas kernels for 0%

commit v1 on v0

--- a/solution.py
+++ b/solution.py
@@ -8,6 +8,12 @@
 rope_theta = 500000.0
 penalty_step = 1.5
 norm_eps = 1e-05
+
+
+def add_all(array, axis):
+    shards = lax.all_gather(array, axis, axis=0, tiled=False)
+    total = shards.sum(axis=0)
+    return total
 
 
 def partner_2(value, axis, distance):
@@ -140,7 +146,7 @@
     recent_mine = lax.dynamic_slice_in_dim(recent_ids, mine_start, half_rows, 0)
     guided = unconditional + guide * (conditional - unconditional)
     guided = guided - penalty_step * repeat_counts(recent_mine, column_base, vocab_local)
-    totals = lax.psum(jnp.sum(jnp.exp(guided), 1), ("dp", "tensor"))
+    totals = add_all(jnp.sum(jnp.exp(guided), 1), ("dp", "tensor"))
     return guided - jnp.log(totals)[:, None]
 
 

time: 648 us -> 501 us (0.77)
  blocking collectives: 427 us -> 275 us
    psum x1 -> x0, blocking collectives: 334 us -> none  [body(): totals = lax.psum(jnp.sum(jnp.exp(guided), 1), ('dp', 'tensor'))]
    all_gather x0 -> x1, blocking collectives: none -> 182 us  [add_all(): shards = lax.all_gather(array, axis, axis=0, tiled=False)]
where the time goes in v1:
time: 501 us; the launch traced here: 495 us
  blocking collectives  275 us (55%)
  waiting for transfers between devices  182 us (36%)
  between operations  13.3 us (3%)
  matrix products  12.1 us (2%)
  other arithmetic  10.7 us (2%)
    all_gather x1, blocking collectives, add_all(): shards = lax.all_gather(array, axis, axis=0, tiled=False)  182 us
    reduce_scatter x1, waiting for transfers between devices, body(): lax.psum_scatter(jnp.concatenate([jnp.dot(all_rows, w_query, preferred_el...  79.2 us
    all_gather x1, waiting for transfers between devices, body(): lax.all_gather(normed_all, 'dp', axis=1, tiled=True)  58.3 us
    psum x1, blocking collectives, body(): squares = lax.psum(jnp.sum(widened * widened, 1), 'dp')  40.3 us
    reduce_scatter x1, waiting for transfers between devices, body(): lax.psum_scatter(partial_out, 'tensor', scatter_dimension=0, tiled=True)  32.9 us
    all_gather x1, blocking collectives, body(): lax.all_gather(attended, 'dp', axis=0, tiled=True)  23.3 us
    all_gather x1, blocking collectives, body(): normed_all = lax.all_gather(normed, 'tensor', axis=0, tiled=True)  15.3 us
    all_gather x1, blocking collectives, body(): all_rows = lax.all_gather(hidden[0], 'tensor', axis=0, tiled=True)  14.5 us
  transfers between devices with their start and end apart: 4, of which 4 were waited for; matrix products, arithmetic and copies ran while one was open for 1% of the time, Pallas kernels for 0%

profile of v1, /device:TPU:128, one launch (start us, length us, event | category | flops | bytes accessed | tf_op | source)
XLA Modules:
  0.0 495.2 jit_solution(4983644203194290432)
XLA Ops:
  6.6 14.5 %all-gather = bf16[1,256,512]{2,1,0:T(8,128)(2,1)S(1)} all-gather(bf16[1,32,512]{2,1,0:T(8,128)(2,1)} %param.11), channel_id=2, replica_groups=mesh['stream'=2,'dp'=16,'tensor'=8] {'tensor'}, dimensions={1}, use_global_device_ids=true | all-gather | bytes 294912 | tf_op jit(solution)/shard_map/all_gather | solution.py:66
  21.1 0.5 fusion.9
  21.6 1.2 fusion.5
  22.8 1.2 pad_maximum_fusion
  24.1 0.7 bitcast_convert_fusion
  24.7 0.7 iota_compare_fusion
  25.6 79.2 %reduce-scatter.3.cloned.1.call-done = f32[16,1280]{1,0:T(8,128)} async-done(((f32[256,1280]{1,0:T(8,128)}), f32[16,1280]{1,0:T(8,128)}) %reduce-scatter.3.cloned.1.call-update) | async-done | bytes 81936 | tf_op jit(solution)/shard_map/reduce_scatter | solution.py:68
  104.8 0.7 slice.36
  105.7 0.8 slice_bitcast_fusion
  106.9 1.7 fusion.33
  108.7 0.3 fusion.2
  109.0 23.3 %all_gather.19 = bf16[256,1024]{1,0:T(8,128)(2,1)S(1)} all-gather(bf16[16,1024]{1,0:T(8,128)(2,1)S(1)} %bitcast.52), channel_id=1, replica_groups=mesh['stream'=2,'dp'=16,'tensor'=8] {'dp'}, dimensions={0}, use_global_device_ids=true | all-gather | bytes 557056 | tf_op jit(solution)/shard_map/all_gather | solution.py:119
  132.3 1.2 fusion.34
  133.6 32.9 %reduce-scatter.5.cloned.1.call-done = f32[32,512]{1,0:T(8,128)} async-done(((f32[256,512]{1,0:T(8,128)}), f32[32,512]{1,0:T(8,128)}) %reduce-scatter.5.cloned.1.call-update) | async-done | bytes 65552 | tf_op jit(solution)/shard_map/reduce_scatter | solution.py:123
  166.5 1.0 fusion.11
  167.5 40.3 %psum.7 = f32[32]{0:T(128)S(1)} all-reduce(f32[32]{0:T(128)S(1)} %fusion.11), channel_id=1, replica_groups=mesh['stream'=2,'dp'=16,'tensor'=8] {'dp'}, use_global_device_ids=true, to_apply=%region_4.5 | all-reduce | flops 32 | bytes 256 | tf_op jit(solution)/shard_map/psum | solution.py:126
  207.8 0.9 fusion.13
  208.7 15.3 %all_gather.20 = bf16[256,512]{1,0:T(8,128)(2,1)} all-gather(bf16[32,512]{1,0:T(8,128)(2,1)S(1)} %fusion.13), channel_id=1, replica_groups=mesh['stream'=2,'dp'=16,'tensor'=8] {'tensor'}, dimensions={0}, use_global_device_ids=true | all-gather | bytes 294912 | tf_op jit(solution)/shard_map/all_gather | solution.py:129
  224.2 58.3 %all-gather.5.cloned.1.call-done = bf16[256,8192]{1,0:T(8,128)(2,1)} async-done(((bf16[256,512]{1,0:T(8,128)(2,1)}), bf16[256,8192]{1,0:T(8,128)(2,1)}) %all-gather.5.cloned.1.call-update) | async-done | bytes 4194320 | tf_op jit(solution)/shard_map/all_gather | solution.py:131
  282.5 7.0 %fusion.35 = f32[256,512]{1,0:T(8,128)S(1)} fusion(bf16[256,8192]{1,0:T(8,128)(2,1)} %all-gather.5.cloned.1.call-done, bf16[8192,512]{1,0:T(8,128)(2,1)} %param.21), kind=kOutput, calls=%fused_computation.66 | convolution fusion | flops 2147483648 | bytes 13107200 | tf_op jit(solution)/shard_map/dot_general | solution.py:130
  289.8 4.7 convert_reduce_fusion
  294.4 11.4 %collective-permute-done = f32[128,512]{1,0:T(8,128)S(1)} collective-permute-done((f32[128,512]{1,0:T(8,128)S(1)}, f32[128,512]{1,0:T(8,128)S(1)}, u32[]{:S(2)}, u32[]{:S(2)}) %collective-permute-start) | collective-permute-done | bytes 262176 | tf_op jit(solution)/shard_map/ppermute | solution.py:22
  306.0 181.7 %all-gather.2 = f32[128,1,128]{2,1,0:T(1,128)S(1)} all-gather(f32[1,1,128]{2,1,0:T(1,128)S(1)} %bitcast.56), channel_id=3, replica_groups=mesh['stream'=2,'dp'=16,'tensor'=8] {'dp','tensor'}, dimensions={0}, use_global_device_ids=true | all-gather | bytes 66048 | tf_op jit(solution)/shard_map/all_gather | solution.py:14
  487.9 0.8 broadcast_subtract_fusion
  (42 shorter events, 1.7 us)
Async XLA Ops:
  6.5 14.6 %copy-start = (bf16[512,1024]{1,0:T(8,128)(2,1)S(1)}, bf16[512,1024]{1,0:T(8,128)(2,1)}, u32[]{:S(2)}) copy-start(bf16[512,1024]{1,0:T(8,128)(2,1)} %param.17) | copy-start | bytes 3145732
  6.5 160.0 %copy-start.3 = (bf16[1,32,512]{2,1,0:T(8,128)(2,1)S(1)}, bf16[1,32,512]{2,1,0:T(8,128)(2,1)}, u32[]{:S(2)}) copy-start(bf16[1,32,512]{2,1,0:T(8,128)(2,1)} %param.11) | copy-start | bytes 98308
  6.5 102.2 %copy-start.1 = (bf16[1,16,1,256,128]{4,3,2,1,0:T(8,128)(2,1)S(1)}, bf16[1,16,1,256,128]{4,3,2,1,0:T(8,128)(2,1)}, u32[]{:S(2)}) copy-start(bf16[1,16,1,256,128]{4,3,2,1,0:T(8,128)(2,1)} %param.13) | copy-start | bytes 3145732
  6.5 125.8 %copy-start.2 = (bf16[1024,512]{1,0:T(8,128)(2,1)S(1)}, bf16[1024,512]{1,0:T(8,128)(2,1)}, u32[]{:S(2)}) copy-start(bf16[1024,512]{1,0:T(8,128)(2,1)} %param.19) | copy-start | bytes 3145732
  6.5 127.1 %copy-start.5 = (bf16[512]{0:T(512)(128)(2,1)S(1)}, bf16[512]{0:T(512)(128)(2,1)}, u32[]{:S(2)}) copy-start(bf16[512]{0:T(512)(128)(2,1)} %param.20) | copy-start | bytes 3076
  6.5 217.5 %copy-start.6 = (f32[256]{0:T(256)S(1)}, f32[256]{0:T(256)}, u32[]{:S(2)}) copy-start(f32[256]{0:T(256)} %param.16) | copy-start | bytes 3076
  6.6 217.6 %copy-start.4 = (s32[256,128]{1,0:T(8,128)S(1)}, s32[256,128]{1,0:T(8,128)}, u32[]{:S(2)}) copy-start(s32[256,128]{1,0:T(8,128)} %param.15) | copy-start | bytes 393220
  6.6 98.2 %reduce-scatter.3.cloned.1.call-start = ((), (), s32[]{:S(2)}) async-start(), calls=%async_computation.2 | async-start | bytes 1392640 | tf_op jit(solution)/shard_map/reduce_scatter | solution.py:68
  24.0 142.5 %reduce-scatter.5.cloned.1.call-start = ((), (), s32[]{:S(2)}) async-start(), calls=%async_computation.3 | async-start | bytes 589824 | tf_op jit(solution)/shard_map/reduce_scatter | solution.py:123
  133.6 148.9 %all-gather.5.cloned.1.call-start = ((), (), s32[]{:S(2)}) async-start(), calls=%async_computation.4 | async-start | bytes 4456448 | tf_op jit(solution)/shard_map/all_gather | solution.py:131
  289.5 16.3 %collective-permute-start = (f32[128,512]{1,0:T(8,128)S(1)}, f32[128,512]{1,0:T(8,128)S(1)}, u32[]{:S(2)}, u32[]{:S(2)}) collective-permute-start(f32[128,512]{1,0:T(8,128)S(1)} %constant_dynamic-slice_fusion.1), channel_id=1, source_target_pairs={{0,128},{128,0},{1,129},{129,1},{2,130},{130,2},{3,131},{131,3},{4... | collective-permute-start | bytes 786440 | tf_op jit(solution)/shard_map/ppermute | solution.py:22
Sparse Core Ops, SparseCore 0:
  24.1 80.6 reduce-scatter.2
  133.7 32.7 reduce-scatter.4
  224.2 58.2 all-gather.4
